TPU v7x, 32 devices: a whole 2x2x4 slice. The times are simulated.
32 devices in a mesh: prow: 8 (over z, y), pcol: 4 (over x, core).
Axes of the slice: x: 2, y: 2, z: 4, core: 2. Of those that a mesh axis runs over, the one named last changes fastest.
Arguments:
- a_panel: float32 [98304, 512], P('prow', 'pcol'), may hold values from -6 to 6
- u_rows: float32 [512, 98304], P('pcol', 'prow'), may hold values from -0.25 to 0.25
- u_col: float32 [98304, 2048], P('prow', 'pcol'), may hold values from -0.01953125 to 0.01953125
- c_in: float32 [98304, 2048], P('prow', 'pcol'), may hold values from -6 to 6
Outputs:
- c_out: float32 [98304, 2048], P('prow', 'pcol')
All inputs are finite; a program needn't handle non-finite values.
Results may differ from a plain program's by a relative error of at most 0.00007.
Values sent between devices are 32-bit elements; how exact they have to be, the bound alone decides.
A program may use at most 192 MiB of HBM per device.

v0:
```python
import jax
import jax.numpy as jnp
from jax import lax
from jax.sharding import PartitionSpec as P


def gather_later(u_rows):
    return lax.all_gather(u_rows, "pcol", axis=0, tiled=True)


def on_device(a_panel, u_rows, u_col, c_in):
    a_full = lax.all_gather(a_panel, "pcol", axis=1, tiled=True)
    partial_inner = jnp.dot(
        a_full.T, u_col, precision=lax.Precision.HIGHEST, preferred_element_type=jnp.float32
    )
    inner = lax.psum(partial_inner, "prow")
    u_full = gather_later(u_rows)
    result = c_in + jnp.dot(
        u_full.T, inner, precision=lax.Precision.HIGHEST, preferred_element_type=jnp.float32
    )
    return result


def solution(mesh):
    placed = (P("prow", "pcol"), P("pcol", "prow"), P("prow", "pcol"), P("prow", "pcol"))
    return jax.shard_map(
        on_device, mesh=mesh, in_specs=placed, out_specs=P("prow", "pcol"), check_vma=False
    )
```

profile of v0, /device:TPU:0, one launch (start us, length us, event | category | flops | bytes accessed | tf_op | source)
XLA Modules:
  0.0 486.4 jit_solution(6694891880605975887)
XLA Ops:
  6.5 0.0 all-gather.3.cloned.1.call-start
  6.5 0.7 all-gather.3.cloned.1.call-update
  7.3 0.0 all-gather.5.cloned.1.call-start
  7.3 0.7 all-gather.5.cloned.1.call-update
  8.0 0.0 all-reduce.2.cloned.1.call-start
  8.1 161.7 %all-gather.3.cloned.1.call-done = f32[12288,512]{1,0:T(8,128)} async-done(((f32[12288,128]{1,0:T(8,128)}), f32[12288,512]{1,0:T(8,128)}) %all-gather.3.cloned.1.call-update) | async-done | bytes 25165840 | tf_op jit(solution)/shard_map/all_gather | solution.py:12
  169.8 45.2 %fusion = f32[512,512]{1,0:T(8,128)} fusion(f32[12288,512]{1,0:T(8,128)} %all-gather.3.cloned.1.call-done, f32[12288,512]{1,0:T(8,128)} %param.6), kind=kOutput, calls=%fused_computation.1 | convolution fusion | flops 38654705664 | bytes 51380224 | tf_op jit(solution)/shard_map/dot_general | solution.py:13
  215.0 0.0 all-reduce.2.cloned.1.call-update
  215.0 24.7 %copy.5 = f32[12288,512]{0,1:T(8,128)} copy(f32[12288,512]{1,0:T(8,128)} %param.7) | data formatting | bytes 50331648 | tf_op args[3]
  239.7 86.5 %all-gather.5.cloned.1.call-done = f32[512,12288]{1,0:T(8,128)} async-done(((f32[128,12288]{1,0:T(8,128)}), f32[512,12288]{1,0:T(8,128)}) %all-gather.5.cloned.1.call-update) | async-done | bytes 25165840 | tf_op jit(solution)/shard_map/all_gather | solution.py:8
  326.2 81.8 %all-reduce.2.cloned.1.call-done = f32[512,512]{1,0:T(8,128)} async-done(((f32[512,512]{1,0:T(8,128)}), f32[512,512]{1,0:T(8,128)}) %all-reduce.2.cloned.1.call-update) | async-done | bytes 1048592 | tf_op jit(solution)/shard_map/psum | solution.py:16
  407.9 47.2 %bitcast_add_fusion = f32[12288,512]{0,1:T(8,128)} fusion(f32[12288,512]{0,1:T(8,128)} %copy.5, f32[512,512]{1,0:T(8,128)} %all-reduce.2.cloned.1.call-done, f32[512,12288]{1,0:T(8,128)} %all-gather.5.cloned.1.call-done), kind=kOutput, calls=%fused_computation | convolution fusion | flops 38660997120 | bytes 76546048 | tf_op jit(solution)/shard_map/dot_general | solution.py:18
  455.2 24.7 %copy.6 = f32[12288,512]{1,0:T(8,128)} copy(f32[12288,512]{0,1:T(8,128)} %bitcast_add_fusion) | data formatting | bytes 50331648 | tf_op jit(solution)/shard_map/add | solution.py:18
Async XLA Ops:
  6.5 163.3 %all-gather.3.cloned.1.call-start = ((), (), s32[]{:S(2)}) async-start(), calls=%async_computation | async-start | bytes 31457280 | tf_op jit(solution)/shard_map/all_gather | solution.py:12
  7.3 318.9 %all-gather.5.cloned.1.call-start = ((), (), s32[]{:S(2)}) async-start(), calls=%async_computation.2 | async-start | bytes 31457280 | tf_op jit(solution)/shard_map/all_gather | solution.py:8
  8.0 399.9 %all-reduce.2.cloned.1.call-start = ((), (), s32[]{:S(2)}) async-start(), calls=%async_computation.1 | async-start | bytes 2097152 | tf_op jit(solution)/shard_map/psum | solution.py:16
Sparse Core Ops, SparseCore 0:
  8.9 160.8 all-gather.2
  171.4 154.7 all-gather.4
  329.7 78.1 all-reduce.1
where the time goes:
time: 487 us; the launch traced here: 486 us
  waiting for transfers between devices  331 us (68%)
  matrix products  92.4 us (19%)
  local copies, waits for them, and re-layouts  49.4 us (10%)
  between operations  13.1 us (3%)
    all_gather x1, waiting for transfers between devices, on_device(): a_full = lax.all_gather(a_panel, 'pcol', axis=1, tiled=True)  162 us
    all_gather x1, waiting for transfers between devices, gather_later(): return lax.all_gather(u_rows, 'pcol', axis=0, tiled=True)  86.5 us
    psum x1, waiting for transfers between devices, on_device(): inner = lax.psum(partial_inner, 'prow')  81.8 us
    dot_general x1, matrix products, on_device(): jnp.dot(u_full.T, inner, precision=lax.Precision.HIGHEST, preferred_eleme...  47.2 us
    dot_general x1, matrix products, on_device(): jnp.dot(a_full.T, u_col, precision=lax.Precision.HIGHEST, preferred_eleme...  45.2 us
    unnamed x1, local copies, waits for them, and re-layouts  24.7 us
    add x1, local copies, waits for them, and re-layouts, on_device(): c_in + jnp.dot(u_full.T, inner, precision=lax.Precision.HIGHEST, preferre...  24.7 us
  transfers between devices with their start and end apart: 3, of which 3 were waited for; matrix products, arithmetic and copies ran while one was open for 14% of the time, Pallas kernels for 0%

commit v1 on v0

--- a/solution.py
+++ b/solution.py
@@ -13,7 +13,7 @@
     partial_inner = jnp.dot(
         a_full.T, u_col, precision=lax.Precision.HIGHEST, preferred_element_type=jnp.float32
     )
-    inner = lax.psum(partial_inner, "prow")
+    inner = jnp.sum(lax.all_gather(partial_inner, "prow"), axis=0)
     u_full = gather_later(u_rows)
     result = c_in + jnp.dot(
         u_full.T, inner, precision=lax.Precision.HIGHEST, preferred_element_type=jnp.float32

time: 487 us -> 573 us (1.18)
  waiting for transfers between devices: 331 us -> 413 us
    all_gather x0 -> x1, waiting for transfers between devices: none -> 99 us  [on_device(): inner = jnp.sum(lax.all_gather(partial_inner, 'prow'), axis=0)]
    psum x1 -> x0, waiting for transfers between devices: 81.8 us -> none  [on_device(): inner = lax.psum(partial_inner, 'prow')]
    all_gather x1, waiting for transfers between devices: 86.5 us -> 150 us  [gather_later(): return lax.all_gather(u_rows, 'pcol', axis=0, tiled=True)]
  transfers between devices with their start and end apart: 3 -> 3, of which waited for: 3 -> 3; matrix products, arithmetic and copies ran while one was open for 14% -> 5% of each run, Pallas kernels for 0% -> 0%
where the time goes in v1:
time: 573 us; the launch traced here: 572 us
  waiting for transfers between devices  413 us (72%)
  matrix products  92.1 us (16%)
  local copies, waits for them, and re-layouts  49.6 us (9%)
  between operations  13.1 us (2%)
    all_gather x1, waiting for transfers between devices, on_device(): a_full = lax.all_gather(a_panel, 'pcol', axis=1, tiled=True)  162 us
    all_gather x1, waiting for transfers between devices, gather_later(): return lax.all_gather(u_rows, 'pcol', axis=0, tiled=True)  150 us
    all_gather x1, waiting for transfers between devices, on_device(): inner = jnp.sum(lax.all_gather(partial_inner, 'prow'), axis=0)  99 us
    dot_general x1, matrix products, on_device(): jnp.dot(u_full.T, inner, precision=lax.Precision.HIGHEST, preferred_eleme...  46.9 us
    dot_general x1, matrix products, on_device(): jnp.dot(a_full.T, u_col, precision=lax.Precision.HIGHEST, preferred_eleme...  45.2 us
    unnamed x1, local copies, waits for them, and re-layouts  24.9 us
    add x1, local copies, waits for them, and re-layouts, on_device(): c_in + jnp.dot(u_full.T, inner, precision=lax.Precision.HIGHEST, preferre...  24.7 us
  transfers between devices with their start and end apart: 3, of which 3 were waited for; matrix products, arithmetic and copies ran while one was open for 5% of the time, Pallas kernels for 0%

profile of v1, /device:TPU:0, one launch (start us, length us, event | category | flops | bytes accessed | tf_op | source)
XLA Modules:
  0.0 572.3 jit_solution(15801662190022713175)
XLA Ops:
  6.5 0.0 all-gather.5.cloned.1.call-start
  6.5 0.7 all-gather.5.cloned.1.call-update
  7.3 0.0 all-gather.9.cloned.1.call-start
  7.3 162.5 %all-gather.5.cloned.1.call-done = f32[12288,512]{1,0:T(8,128)} async-done(((f32[12288,128]{1,0:T(8,128)}), f32[12288,512]{1,0:T(8,128)}) %all-gather.5.cloned.1.call-update) | async-done | bytes 25165840 | tf_op jit(solution)/shard_map/all_gather | solution.py:12
  169.8 45.2 %fusion = f32[512,512]{1,0:T(8,128)} fusion(f32[12288,512]{1,0:T(8,128)} %all-gather.5.cloned.1.call-done, f32[12288,512]{1,0:T(8,128)} %param.6), kind=kOutput, calls=%fused_computation.1 | convolution fusion | flops 38654705664 | bytes 51380224 | tf_op jit(solution)/shard_map/dot_general | solution.py:13
  215.0 0.0 all-gather.9.cloned.1.call-update
  215.0 0.2 all-gather.7.cloned.1.call-start
  215.2 0.5 all-gather.7.cloned.1.call-update
  215.7 24.9 %copy.5 = f32[12288,512]{0,1:T(8,128)} copy(f32[12288,512]{1,0:T(8,128)} %param.7) | data formatting | bytes 50331648 | tf_op args[3]
  240.6 99.0 %all-gather.9.cloned.1.call-done = f32[4096,512]{1,0:T(8,128)} async-done(((f32[512,512]{1,0:T(8,128)}), f32[4096,512]{1,0:T(8,128)}) %all-gather.9.cloned.1.call-update) | async-done | bytes 8388624 | tf_op jit(solution)/shard_map/all_gather | solution.py:16
  339.6 4.5 reduce_sum.9
  344.1 150.1 %all-gather.7.cloned.1.call-done = f32[512,12288]{1,0:T(8,128)} async-done(((f32[128,12288]{1,0:T(8,128)}), f32[512,12288]{1,0:T(8,128)}) %all-gather.7.cloned.1.call-update) | async-done | bytes 25165840 | tf_op jit(solution)/shard_map/all_gather | solution.py:8
  494.2 46.9 %bitcast_add_fusion = f32[12288,512]{0,1:T(8,128)} fusion(f32[12288,512]{0,1:T(8,128)} %copy.5, f32[512,512]{1,0:T(8,128)S(1)} %reduce_sum.9, f32[512,12288]{1,0:T(8,128)} %all-gather.7.cloned.1.call-done), kind=kOutput, calls=%fused_computation | convolution fusion | flops 38660997120 | bytes 76546048 | tf_op jit(solution)/shard_map/dot_general | solution.py:18
  541.1 24.7 %copy.6 = f32[12288,512]{1,0:T(8,128)} copy(f32[12288,512]{0,1:T(8,128)} %bitcast_add_fusion) | data formatting | bytes 50331648 | tf_op jit(solution)/shard_map/add | solution.py:18
Async XLA Ops:
  6.5 163.3 %all-gather.5.cloned.1.call-start = ((), (), s32[]{:S(2)}) async-start(), calls=%async_computation | async-start | bytes 31457280 | tf_op jit(solution)/shard_map/all_gather | solution.py:12
  7.3 332.4 %all-gather.9.cloned.1.call-start = ((), (), s32[]{:S(2)}) async-start(), calls=%async_computation.2 | async-start | bytes 9437184 | tf_op jit(solution)/shard_map/all_gather | solution.py:16
  215.0 279.2 %all-gather.7.cloned.1.call-start = ((), (), s32[]{:S(2)}) async-start(), calls=%async_computation.1 | async-start | bytes 31457280 | tf_op jit(solution)/shard_map/all_gather | solution.py:8
Sparse Core Ops, SparseCore 0:
  8.9 160.8 all-gather.4
  215.1 124.4 all-gather.8
  341.2 152.9 all-gather.6
